TPU v7x, 256 devices: a whole 4x4x8 slice. The times are simulated.
256 devices in a mesh: dp: 64 (over z, y, x_hi), seq: 4 (over x_lo, core).
Axes of the slice: x: 4 (x_hi: 2, x_lo: 2; x = x_hi * 2 + x_lo), y: 4, z: 8, core: 2. Of those that a mesh axis runs over, the one named last changes fastest.
Arguments:
- queries: bfloat16 [32768, 2560], P(('dp', 'seq')), may hold values from -400 to 400
- key_states: bfloat16 [32768, 2560], P(('dp', 'seq')), may hold values from -400 to 400
- value_states: bfloat16 [32768, 2560], P(('dp', 'seq')), may hold values from -6 to 6
- query_tangent: bfloat16 [32768, 2560], P(('dp', 'seq')), may hold values from -6 to 6
- key_tangent: bfloat16 [32768, 2560], P(('dp', 'seq')), may hold values from -6 to 6
- value_tangent: bfloat16 [32768, 2560], P(('dp', 'seq')), may hold values from -6 to 6
- query_gain: float32 [2560], replicated, may hold values from 0.25 to 1.75
- key_gain: float32 [2560], replicated, may hold values from 0.25 to 1.75
- out_weight: bfloat16 [2560, 5120], P('seq', 'dp'), may hold values from -0.125 to 0.125
Outputs:
- projected: bfloat16 [32768, 5120], P(('dp', 'seq'))
- projected_tangent: bfloat16 [32768, 5120], P(('dp', 'seq'))
All inputs are finite; a program needn't handle non-finite values.
Results may differ from a plain program's by a relative error of at most 0.012.
The roundings to bfloat16 on the way count: a program that leaves them out, or rounds other values in their place, can miss the bound.
Values may be sent and summed in bfloat16 or wider, within the bound.
A program may use at most 128 MiB of HBM per device.

v0:
```python
import jax
import jax.numpy as jnp
from jax import lax
from jax.sharding import PartitionSpec as P

HEADS = 20
HDIM = 128


def rms_tangent(primal, tangent, gain):
    primal_f = primal.astype(jnp.float32)
    tangent_f = tangent.astype(jnp.float32)
    inverse = lax.rsqrt(jnp.mean(primal_f * primal_f, axis=-1, keepdims=True) + 1e-06)
    across = jnp.mean(primal_f * tangent_f, axis=-1, keepdims=True)
    normed = (primal_f * inverse * gain).astype(jnp.bfloat16)
    normed_tangent = (gain * (tangent_f * inverse - primal_f * inverse**3 * across)).astype(
        jnp.bfloat16
    )
    return (normed, normed_tangent)


def attend(query_normed, query_dual, key_normed, key_dual, value_plain, value_dual):
    factor = HDIM ** (-0.5)
    scores = (
        jnp.einsum("qhd,khd->hqk", query_normed, key_normed, preferred_element_type=jnp.float32)
        * factor
    )
    dual_scores = (
        jnp.einsum("qhd,khd->hqk", query_dual, key_normed, preferred_element_type=jnp.float32)
        + jnp.einsum("qhd,khd->hqk", query_normed, key_dual, preferred_element_type=jnp.float32)
    ) * factor
    peak = jnp.max(scores, axis=-1, keepdims=True)
    raised = jnp.exp(scores - peak)
    probs = raised / jnp.sum(raised, axis=-1, keepdims=True)
    spread = probs * (dual_scores - jnp.sum(probs * dual_scores, axis=-1, keepdims=True))
    probs_low = probs.astype(jnp.bfloat16)
    spread_low = spread.astype(jnp.bfloat16)
    attn = jnp.einsum(
        "hqk,khd->qhd", probs_low, value_plain, preferred_element_type=jnp.float32
    ).astype(jnp.bfloat16)
    dual_attn = (
        jnp.einsum("hqk,khd->qhd", probs_low, value_dual, preferred_element_type=jnp.float32)
        + jnp.einsum("hqk,khd->qhd", spread_low, value_plain, preferred_element_type=jnp.float32)
    ).astype(jnp.bfloat16)
    return (attn, dual_attn)


def body(
    queries,
    key_states,
    value_states,
    query_tangent,
    key_tangent,
    value_tangent,
    query_gain,
    key_gain,
    out_weight,
):
    rows_here = queries.shape[0]
    query_normed, query_dual = rms_tangent(queries, query_tangent, query_gain)
    key_normed, key_dual = rms_tangent(key_states, key_tangent, key_gain)
    by_head = (
        lax.all_to_all(
            query_normed.reshape(rows_here, HEADS, HDIM),
            "seq",
            split_axis=1,
            concat_axis=0,
            tiled=True,
        ),
        lax.all_to_all(
            query_dual.reshape(rows_here, HEADS, HDIM),
            "seq",
            split_axis=1,
            concat_axis=0,
            tiled=True,
        ),
        lax.all_to_all(
            key_normed.reshape(rows_here, HEADS, HDIM),
            "seq",
            split_axis=1,
            concat_axis=0,
            tiled=True,
        ),
        lax.all_to_all(
            key_dual.reshape(rows_here, HEADS, HDIM), "seq", split_axis=1, concat_axis=0, tiled=True
        ),
        lax.all_to_all(
            value_states.reshape(rows_here, HEADS, HDIM),
            "seq",
            split_axis=1,
            concat_axis=0,
            tiled=True,
        ),
        lax.all_to_all(
            value_tangent.reshape(rows_here, HEADS, HDIM),
            "seq",
            split_axis=1,
            concat_axis=0,
            tiled=True,
        ),
    )
    attn, dual_attn = attend(by_head[0], by_head[1], by_head[2], by_head[3], by_head[4], by_head[5])
    width_all = HEADS * HDIM
    back_plain, back_dual = (
        lax.all_to_all(attn, "seq", split_axis=0, concat_axis=1, tiled=True),
        lax.all_to_all(dual_attn, "seq", split_axis=0, concat_axis=1, tiled=True),
    )
    stacked = jnp.concatenate(
        [back_plain.reshape(rows_here, width_all), back_dual.reshape(rows_here, width_all)], axis=0
    )
    full_rows = lax.all_gather(out_weight, "seq", axis=0, tiled=True)
    result = jnp.dot(
        stacked,
        lax.all_gather(full_rows, "dp", axis=1, tiled=True),
        preferred_element_type=jnp.float32,
    ).astype(jnp.bfloat16)
    return (result[:rows_here], result[rows_here:])


def solution(mesh):
    return jax.shard_map(
        body,
        mesh=mesh,
        in_specs=(
            P(("dp", "seq"), None),
            P(("dp", "seq"), None),
            P(("dp", "seq"), None),
            P(("dp", "seq"), None),
            P(("dp", "seq"), None),
            P(("dp", "seq"), None),
            P(),
            P(),
            P("seq", "dp"),
        ),
        out_specs=(P(("dp", "seq"), None), P(("dp", "seq"), None)),
        check_vma=False,
    )
```

profile of v0, /device:TPU:24, one launch (start us, length us, event | category | flops | bytes accessed | tf_op | source)
XLA Modules:
  0.0 334.1 jit_solution(1563490094878376542)
XLA Ops:
  7.2 8.2 %all_gather.6 = bf16[2560,80]{0,1:T(8,128)(2,1)} all-gather(bf16[640,80]{0,1:T(8,128)(2,1)} %param.17), channel_id=1, replica_groups=mesh['dp'=64,'seq'=4] {'seq'}, dimensions={0}, use_global_device_ids=true | all-gather | bytes 512000 | tf_op jit(solution)/shard_map/all_gather | solution.py:111
  19.3 3.6 %all-to-all-start.1 = ((bf16[128,20,128]{0,2,1:T(8,128)(2,1)}), bf16[128,20,128]{0,2,1:T(8,128)(2,1)S(1)}, u32[]{:S(2)}, u32[]{:S(2)}) async-start(bf16[128,20,128]{0,2,1:T(8,128)(2,1)} %bitcast.5), calls=%async_computation.1 | async-start | bytes 1310720 | tf_op jit(solution)/shard_map/all_to_all | solution.py:77
  25.4 7.7 %all-to-all-done.1 = bf16[128,20,128]{0,2,1:T(8,128)(2,1)S(1)} async-done(((bf16[128,20,128]{0,2,1:T(8,128)(2,1)}), bf16[128,20,128]{0,2,1:T(8,128)(2,1)S(1)}, u32[]{:S(2)}, u32[]{:S(2)}) %all-to-all-start.1) | async-done | bytes 655392 | tf_op jit(solution)/shard_map/all_to_all | solution.py:77
  33.1 3.5 %all-to-all-start = ((bf16[128,20,128]{0,2,1:T(8,128)(2,1)}), bf16[128,20,128]{0,2,1:T(8,128)(2,1)S(1)}, u32[]{:S(2)}, u32[]{:S(2)}) async-start(bf16[128,20,128]{0,2,1:T(8,128)(2,1)} %bitcast.68), calls=%async_computation | async-start | bytes 1310720 | tf_op jit(solution)/shard_map/all_to_all | solution.py:63
  38.0 8.8 %all-to-all-done = bf16[128,20,128]{0,2,1:T(8,128)(2,1)S(1)} async-done(((bf16[128,20,128]{0,2,1:T(8,128)(2,1)}), bf16[128,20,128]{0,2,1:T(8,128)(2,1)S(1)}, u32[]{:S(2)}, u32[]{:S(2)}) %all-to-all-start) | async-done | bytes 655392 | tf_op jit(solution)/shard_map/all_to_all | solution.py:63
  46.8 13.3 %all_to_all.138 = bf16[128,20,128]{0,2,1:T(8,128)(2,1)} all-to-all(bf16[128,20,128]{0,2,1:T(8,128)(2,1)S(1)} %bitcast.65), channel_id=1, replica_groups=mesh['dp'=64,'seq'=4] {'seq'}, dimensions={1} | all-to-all | bytes 1310720 | tf_op jit(solution)/shard_map/all_to_all | solution.py:87
  60.1 13.4 %all_to_all.139 = bf16[128,20,128]{0,2,1:T(8,128)(2,1)S(1)} all-to-all(bf16[128,20,128]{0,2,1:T(8,128)(2,1)S(1)} %bitcast.67), channel_id=1, replica_groups=mesh['dp'=64,'seq'=4] {'seq'}, dimensions={1} | all-to-all | bytes 1310720 | tf_op jit(solution)/shard_map/all_to_all | solution.py:70
  73.5 3.5 %all-to-all-start.6 = ((bf16[128,20,128]{0,2,1:T(8,128)(2,1)}), bf16[128,20,128]{0,2,1:T(8,128)(2,1)S(1)}, u32[]{:S(2)}, u32[]{:S(2)}) async-start(bf16[128,20,128]{0,2,1:T(8,128)(2,1)} %bitcast.66), calls=%async_computation.6 | async-start | bytes 1310720 | tf_op jit(solution)/shard_map/all_to_all | solution.py:84
  76.9 2.2 copy.73
  79.8 1.6 copy.68
  81.5 4.1 %fusion.40 = (f32[5,512]{1,0:T(8,128)S(1)}, f32[5,512,512]{1,2,0:T(8,128)}) fusion(bf16[512,5,128]{2,0,1:T(8,128)(2,1)S(1)} %bitcast.71, bf16[512,5,128]{2,0,1:T(8,128)(2,1)S(1)} %bitcast.56), kind=kOutput, calls=%fused_computation.59 | convolution fusion | flops 339476992 | bytes 6563840 | tf_op jit(solution)/shard_map/sub | solution.py:33
  85.6 9.0 %all-to-all-done.6 = bf16[128,20,128]{0,2,1:T(8,128)(2,1)S(1)} async-done(((bf16[128,20,128]{0,2,1:T(8,128)(2,1)}), bf16[128,20,128]{0,2,1:T(8,128)(2,1)S(1)}, u32[]{:S(2)}, u32[]{:S(2)}) %all-to-all-start.6) | async-done | bytes 655392 | tf_op jit(solution)/shard_map/all_to_all | solution.py:84
  94.6 3.5 %all-to-all-start.4 = ((bf16[128,20,128]{0,2,1:T(8,128)(2,1)}), bf16[128,20,128]{0,2,1:T(8,128)(2,1)S(1)}, u32[]{:S(2)}, u32[]{:S(2)}) async-start(bf16[128,20,128]{0,2,1:T(8,128)(2,1)} %bitcast.20), calls=%async_computation.4 | async-start | bytes 1310720 | tf_op jit(solution)/shard_map/all_to_all | solution.py:94
  98.1 3.6 %fusion.32 = bf16[512,5,128]{2,0,1:T(8,128)(2,1)S(1)} fusion(bf16[512,5,128]{2,0,1:T(8,128)(2,1)S(1)} %bitcast.69, f32[5,512,512]{1,2,0:T(8,128)} %get-tuple-element.17, f32[5,512]{1,0:T(8,128)S(1)} %get-tuple-element.16), kind=kOutput, calls=%fused_computation.48 | convolution fusion | flops 338493440 | bytes 6563840 | tf_op jit(solution)/shard_map/hqk,khd->qhd/dot_general | solution.py:38
  104.6 5.5 %all-to-all-done.4 = bf16[128,20,128]{0,2,1:T(8,128)(2,1)S(1)} async-done(((bf16[128,20,128]{0,2,1:T(8,128)(2,1)}), bf16[128,20,128]{0,2,1:T(8,128)(2,1)S(1)}, u32[]{:S(2)}, u32[]{:S(2)}) %all-to-all-start.4) | async-done | bytes 655392 | tf_op jit(solution)/shard_map/all_to_all | solution.py:94
  110.1 3.7 %all-to-all-start.3 = ((bf16[512,5,128]{2,1,0:T(8,128)(2,1)}), bf16[512,5,128]{2,1,0:T(8,128)(2,1)S(1)}, u32[]{:S(2)}, u32[]{:S(2)}) async-start(bf16[512,5,128]{2,1,0:T(8,128)(2,1)} %copy.70), calls=%async_computation.3 | async-start | bytes 2097152 | tf_op jit(solution)/shard_map/all_to_all | solution.py:105
  116.0 1.7 copy-done.11
  119.0 1.8 multiply_reduce_fusion
  123.6 4.5 %all-to-all-done.3 = bf16[512,5,128]{2,1,0:T(8,128)(2,1)S(1)} async-done(((bf16[512,5,128]{2,1,0:T(8,128)(2,1)}), bf16[512,5,128]{2,1,0:T(8,128)(2,1)S(1)}, u32[]{:S(2)}, u32[]{:S(2)}) %all-to-all-start.3) | async-done | bytes 655392 | tf_op jit(solution)/shard_map/all_to_all | solution.py:105
  128.0 3.5 %all-to-all-start.7 = ((bf16[512,5,128]{2,1,0:T(8,128)(2,1)}), bf16[512,5,128]{2,1,0:T(8,128)(2,1)S(1)}, u32[]{:S(2)}, u32[]{:S(2)}) async-start(bf16[512,5,128]{2,1,0:T(8,128)(2,1)} %copy.84), calls=%async_computation.7 | async-start | bytes 2097152 | tf_op jit(solution)/shard_map/all_to_all | solution.py:106
  132.2 13.8 %all-to-all-done.7 = bf16[512,5,128]{2,1,0:T(8,128)(2,1)S(1)} async-done(((bf16[512,5,128]{2,1,0:T(8,128)(2,1)}), bf16[512,5,128]{2,1,0:T(8,128)(2,1)S(1)}, u32[]{:S(2)}, u32[]{:S(2)}) %all-to-all-start.7) | async-done | bytes 655392 | tf_op jit(solution)/shard_map/all_to_all | solution.py:106
  147.2 166.1 %all-gather.2.cloned.1.call-done = bf16[2560,5120]{0,1:T(8,128)(2,1)} async-done(((bf16[2560,80]{0,1:T(8,128)(2,1)}), bf16[2560,5120]{0,1:T(8,128)(2,1)}) %all-gather.2.cloned.1.call-update) | async-done | bytes 26214416 | tf_op jit(solution)/shard_map/all_gather | solution.py:114
  313.3 12.3 %convolution_convert_fusion = bf16[256,5120]{1,0:T(8,128)(2,1)S(1)} fusion(bf16[2560,5120]{0,1:T(8,128)(2,1)} %all-gather.2.cloned.1.call-done, bf16[128,2560]{0,1:T(8,128)(2,1)} %bitcast.75, bf16[128,2560]{0,1:T(8,128)(2,1)S(1)} %bitcast.74), kind=kOutput, calls=%fused_computation.1 | convolution fusion | flops 6714818560 | bytes 30146560 | tf_op jit(solution)/shard_map/dot_general | solution.py:112
  325.6 1.7 fusion.39
  (48 shorter events, 19.4 us)
Async XLA Ops:
  7.2 9.7 %copy-start = (bf16[128,2560]{1,0:T(8,128)(2,1)S(1)}, bf16[128,2560]{1,0:T(8,128)(2,1)}, u32[]{:S(2)}) copy-start(bf16[128,2560]{1,0:T(8,128)(2,1)} %param.13) | copy-start | bytes 1966084
  7.2 10.5 %copy-start.9 = (f32[2560]{0:T(1024)S(1)}, f32[2560]{0:T(1024)}, u32[]{:S(2)}) copy-start(f32[2560]{0:T(1024)} %param.16) | copy-start | bytes 30724
  7.2 306.1 %all-gather.2.cloned.1.call-start = ((), (), s32[]{:S(2)}) async-start(), calls=%async_computation.8 | async-start | bytes 26624000 | tf_op jit(solution)/shard_map/all_gather | solution.py:114
  17.2 5.7 %copy-start.1 = (bf16[128,2560]{1,0:T(8,128)(2,1)S(1)}, bf16[128,2560]{1,0:T(8,128)(2,1)}, u32[]{:S(2)}) copy-start(bf16[128,2560]{1,0:T(8,128)(2,1)} %param.9) | copy-start | bytes 1966084
  17.7 5.6 %copy-start.2 = (bf16[128,2560]{1,0:T(8,128)(2,1)S(1)}, bf16[128,2560]{1,0:T(8,128)(2,1)}, u32[]{:S(2)}) copy-start(bf16[128,2560]{1,0:T(8,128)(2,1)} %param.12) | copy-start | bytes 1966084
  19.3 4.7 %copy-start.10 = (f32[2560]{0:T(1024)S(1)}, f32[2560]{0:T(1024)}, u32[]{:S(2)}) copy-start(f32[2560]{0:T(1024)} %param.15) | copy-start | bytes 30724
  19.3 13.8 %all-to-all-start.1 = ((bf16[128,20,128]{0,2,1:T(8,128)(2,1)}), bf16[128,20,128]{0,2,1:T(8,128)(2,1)S(1)}, u32[]{:S(2)}, u32[]{:S(2)}) async-start(bf16[128,20,128]{0,2,1:T(8,128)(2,1)} %bitcast.5), calls=%async_computation.1 | async-start | bytes 1310720 | tf_op jit(solution)/shard_map/all_to_all | solution.py:77
  33.1 13.7 %all-to-all-start = ((bf16[128,20,128]{0,2,1:T(8,128)(2,1)}), bf16[128,20,128]{0,2,1:T(8,128)(2,1)S(1)}, u32[]{:S(2)}, u32[]{:S(2)}) async-start(bf16[128,20,128]{0,2,1:T(8,128)(2,1)} %bitcast.68), calls=%async_computation | async-start | bytes 1310720 | tf_op jit(solution)/shard_map/all_to_all | solution.py:63
  73.5 21.1 %all-to-all-start.6 = ((bf16[128,20,128]{0,2,1:T(8,128)(2,1)}), bf16[128,20,128]{0,2,1:T(8,128)(2,1)S(1)}, u32[]{:S(2)}, u32[]{:S(2)}) async-start(bf16[128,20,128]{0,2,1:T(8,128)(2,1)} %bitcast.66), calls=%async_computation.6 | async-start | bytes 1310720 | tf_op jit(solution)/shard_map/all_to_all | solution.py:84
  79.8 5.8 %copy-start.5 = (bf16[4,128,5,128]{3,1,0,2:T(8,128)(2,1)}, bf16[4,128,5,128]{3,1,0,2:T(8,128)(2,1)S(1)}, u32[]{:S(2)}) copy-start(bf16[4,128,5,128]{3,1,0,2:T(8,128)(2,1)S(1)} %copy.62) | copy-start | bytes 1966084
  81.5 16.6 %copy-start.3 = (bf16[4,128,5,128]{3,1,0,2:T(8,128)(2,1)}, bf16[4,128,5,128]{3,1,0,2:T(8,128)(2,1)S(1)}, u32[]{:S(2)}) copy-start(bf16[4,128,5,128]{3,1,0,2:T(8,128)(2,1)S(1)} %copy.68) | copy-start | bytes 1966084
  94.6 15.5 %all-to-all-start.4 = ((bf16[128,20,128]{0,2,1:T(8,128)(2,1)}), bf16[128,20,128]{0,2,1:T(8,128)(2,1)S(1)}, u32[]{:S(2)}, u32[]{:S(2)}) async-start(bf16[128,20,128]{0,2,1:T(8,128)(2,1)} %bitcast.20), calls=%async_computation.4 | async-start | bytes 1310720 | tf_op jit(solution)/shard_map/all_to_all | solution.py:94
  110.1 17.9 %all-to-all-start.3 = ((bf16[512,5,128]{2,1,0:T(8,128)(2,1)}), bf16[512,5,128]{2,1,0:T(8,128)(2,1)S(1)}, u32[]{:S(2)}, u32[]{:S(2)}) async-start(bf16[512,5,128]{2,1,0:T(8,128)(2,1)} %copy.70), calls=%async_computation.3 | async-start | bytes 2097152 | tf_op jit(solution)/shard_map/all_to_all | solution.py:105
  114.9 1.1 copy-start.8
  114.9 2.8 copy-start.11
  117.6 1.1 copy-start.6
  117.7 1.3 copy-start.7
  119.0 1.8 copy-start.4
  128.0 17.9 %all-to-all-start.7 = ((bf16[512,5,128]{2,1,0:T(8,128)(2,1)}), bf16[512,5,128]{2,1,0:T(8,128)(2,1)S(1)}, u32[]{:S(2)}, u32[]{:S(2)}) async-start(bf16[512,5,128]{2,1,0:T(8,128)(2,1)} %copy.84), calls=%async_computation.7 | async-start | bytes 2097152 | tf_op jit(solution)/shard_map/all_to_all | solution.py:106
Sparse Core Ops, SparseCore 0:
  15.6 297.6 all-gather.1
where the time goes:
time: 335 us; the launch traced here: 334 us
  waiting for transfers between devices  215 us (64%)
  blocking collectives  34.9 us (10%)
  matrix products  25 us (7%)
  starting transfers between devices  21.3 us (6%)
  local copies, waits for them, and re-layouts  19.5 us (6%)
  between operations  14.3 us (4%)
  other arithmetic  3.83 us (1%)
    all_gather x1, waiting for transfers between devices, body(): lax.all_gather(full_rows, 'dp', axis=1, tiled=True)  166 us
    all_to_all x1, waiting for transfers between devices, body(): lax.all_to_all(dual_attn, 'seq', split_axis=0, concat_axis=1, tiled=True)  13.8 us
    all_to_all x1, blocking collectives, body(): lax.all_to_all(query_dual.reshape(rows_here, HEADS, HDIM), 'seq', split_a...  13.4 us
    all_to_all x1, blocking collectives, body(): lax.all_to_all(value_states.reshape(rows_here, HEADS, HDIM), 'seq', split...  13.3 us
    dot_general x1, matrix products, body(): jnp.dot(stacked, lax.all_gather(full_rows, 'dp', axis=1, tiled=True), pre...  12.3 us
    all_to_all x1, waiting for transfers between devices, body(): lax.all_to_all(key_dual.reshape(rows_here, HEADS, HDIM), 'seq', split_axi...  8.99 us
    all_to_all x1, waiting for transfers between devices, body(): lax.all_to_all(query_normed.reshape(rows_here, HEADS, HDIM), 'seq', split...  8.77 us
    all_gather x1, blocking collectives, body(): full_rows = lax.all_gather(out_weight, 'seq', axis=0, tiled=True)  8.24 us
  transfers between devices with their start and end apart: 7, of which 7 were waited for; matrix products, arithmetic and copies ran while one was open for 10% of the time, Pallas kernels for 0%

commit v1 on v0

--- a/solution.py
+++ b/solution.py
@@ -111,7 +111,9 @@
     full_rows = lax.all_gather(out_weight, "seq", axis=0, tiled=True)
     result = jnp.dot(
         stacked,
-        lax.all_gather(full_rows, "dp", axis=1, tiled=True),
+        jnp.concatenate(
+            lax.all_to_all(jnp.stack([full_rows] * lax.axis_size("dp")), "dp", 0, 0), axis=1
+        ),
         preferred_element_type=jnp.float32,
     ).astype(jnp.bfloat16)
     return (result[:rows_here], result[rows_here:])

time: 335 us -> 844 us (2.52)
  the two profiles are of different devices: /device:TPU:24 before, /device:TPU:248 now
where the time goes in v1:
time: 844 us; the launch traced here: 843 us
  waiting for transfers between devices  710 us (84%)
  starting transfers between devices  36.3 us (4%)
  matrix products  33.1 us (4%)
  blocking collectives  30 us (4%)
  local copies, waits for them, and re-layouts  28 us (3%)
    all_to_all x1, waiting for transfers between devices, body(): lax.all_to_all(jnp.stack([full_rows] * lax.axis_size('dp')), 'dp', 0, 0)  671 us
    all_gather x1, blocking collectives, body(): full_rows = lax.all_gather(out_weight, 'seq', axis=0, tiled=True)  17.4 us
  transfers between devices with their start and end apart: 8, of which 6 were waited for; matrix products, arithmetic and copies ran while one was open for 3% of the time, Pallas kernels for 0%

profile of v1, /device:TPU:248, one launch (start us, length us, event | category | flops | bytes accessed | tf_op | source)
XLA Modules:
  0.0 842.7 jit_solution(5476868527706338523)
XLA Ops:
  0.6 2.3 copy.74
  2.9 3.5 all-to-all-start.4
  12.4 4.2 all-to-all-done.4
  16.6 3.5 all-to-all-start
  21.7 8.6 %all-to-all-done = bf16[128,20,128]{0,2,1:T(8,128)(2,1)S(1)} async-done(((bf16[128,20,128]{0,2,1:T(8,128)(2,1)}), bf16[128,20,128]{0,2,1:T(8,128)(2,1)S(1)}, u32[]{:S(2)}, u32[]{:S(2)}) %all-to-all-start) | async-done | bytes 655392 | tf_op jit(solution)/shard_map/all_to_all | solution.py:63
  30.3 3.5 all-to-all-start.1
  35.2 8.8 %all-to-all-done.1 = bf16[128,20,128]{0,2,1:T(8,128)(2,1)S(1)} async-done(((bf16[128,20,128]{0,2,1:T(8,128)(2,1)}), bf16[128,20,128]{0,2,1:T(8,128)(2,1)S(1)}, u32[]{:S(2)}, u32[]{:S(2)}) %all-to-all-start.1) | async-done | bytes 655392 | tf_op jit(solution)/shard_map/all_to_all | solution.py:77
  43.9 12.6 %all_to_all.143 = bf16[128,20,128]{0,2,1:T(8,128)(2,1)S(1)} all-to-all(bf16[128,20,128]{0,2,1:T(8,128)(2,1)S(1)} %bitcast.70), channel_id=1, replica_groups=mesh['dp'=64,'seq'=4] {'seq'}, dimensions={1} | all-to-all | bytes 1310720 | tf_op jit(solution)/shard_map/all_to_all | solution.py:87
  56.6 3.5 all-to-all-start.5
  61.5 8.7 %all-to-all-done.5 = bf16[128,20,128]{0,2,1:T(8,128)(2,1)S(1)} async-done(((bf16[128,20,128]{0,2,1:T(8,128)(2,1)}), bf16[128,20,128]{0,2,1:T(8,128)(2,1)S(1)}, u32[]{:S(2)}, u32[]{:S(2)}) %all-to-all-start.5) | async-done | bytes 655392 | tf_op jit(solution)/shard_map/all_to_all | solution.py:70
  70.2 3.7 all-to-all-start.6
  73.9 5.2 fusion.40
  81.6 3.2 fusion.41
  85.9 3.8 fusion.28
  90.2 3.8 multiply_reduce_fusion
  96.8 3.5 all-to-all-start.7
  100.3 3.5 fusion.32
  105.3 9.4 %all-to-all-done.7 = bf16[512,5,128]{2,1,0:T(8,128)(2,1)S(1)} async-done(((bf16[512,5,128]{2,1,0:T(8,128)(2,1)}), bf16[512,5,128]{2,1,0:T(8,128)(2,1)S(1)}, u32[]{:S(2)}, u32[]{:S(2)}) %all-to-all-start.7) | async-done | bytes 655392 | tf_op jit(solution)/shard_map/all_to_all | solution.py:106
  114.7 3.5 all-to-all-start.3
  118.3 17.4 %all_gather.3 = bf16[2560,80]{0,1:T(8,128)(2,1)S(1)} all-gather(bf16[640,80]{0,1:T(8,128)(2,1)S(1)} %copy-done.5), channel_id=1, replica_groups=mesh['dp'=64,'seq'=4] {'seq'}, dimensions={0}, use_global_device_ids=true | all-gather | bytes 512000 | tf_op jit(solution)/shard_map/all_gather | solution.py:111
  135.7 8.8 %stack.2 = bf16[64,2560,80]{1,2,0:T(8,128)(2,1)} broadcast(bf16[2560,80]{0,1:T(8,128)(2,1)S(1)} %all_gather.3), dimensions={1,2} | broadcast | bytes 26624000 | tf_op jit(solution)/shard_map/stack | solution.py:115
  144.5 11.6 %all-to-all-start.8 = ((bf16[64,2560,80]{1,2,0:T(8,128)(2,1)}), bf16[64,2560,80]{1,2,0:T(8,128)(2,1)}, u32[]{:S(2)}, u32[]{:S(2)}) async-start(bf16[64,2560,80]{1,2,0:T(8,128)(2,1)} %stack.2), calls=%async_computation.8 | async-start | bytes 52428800 | tf_op jit(solution)/shard_map/all_to_all | solution.py:115
  158.1 670.6 %all-to-all-done.8 = bf16[64,2560,80]{1,2,0:T(8,128)(2,1)} async-done(((bf16[64,2560,80]{1,2,0:T(8,128)(2,1)}), bf16[64,2560,80]{1,2,0:T(8,128)(2,1)}, u32[]{:S(2)}, u32[]{:S(2)}) %all-to-all-start.8) | async-done | bytes 26214432 | tf_op jit(solution)/shard_map/all_to_all | solution.py:115
  828.8 12.3 %convolution_convert_fusion = bf16[256,5120]{1,0:T(8,128)(2,1)S(1)} fusion(bf16[2560,5120]{0,1:T(8,128)(2,1)} %bitcast.41, bf16[128,2560]{0,1:T(8,128)(2,1)S(1)} %bitcast.80, bf16[128,2560]{0,1:T(8,128)(2,1)} %bitcast.82), kind=kOutput, calls=%fused_computation.1 | convolution fusion | flops 6714818560 | bytes 30146560 | tf_op jit(solution)/shard_map/dot_general | solution.py:112
  (51 shorter events, 22.2 us)
Async XLA Ops:
  0.6 5.8 copy-start
  0.6 6.1 copy-start.1
  2.9 13.7 %all-to-all-start.4 = ((bf16[128,20,128]{0,2,1:T(8,128)(2,1)}), bf16[128,20,128]{0,2,1:T(8,128)(2,1)S(1)}, u32[]{:S(2)}, u32[]{:S(2)}) async-start(bf16[128,20,128]{0,2,1:T(8,128)(2,1)} %bitcast.20), calls=%async_computation.4 | async-start | bytes 1310720 | tf_op jit(solution)/shard_map/all_to_all | solution.py:94
  7.1 3.7 copy-start.6
  10.3 9.7 %copy-start.7 = (f32[2560]{0:T(1024)S(1)}, f32[2560]{0:T(1024)}, u32[]{:S(2)}) copy-start(f32[2560]{0:T(1024)} %param.16) | copy-start | bytes 30724
  16.6 13.7 %all-to-all-start = ((bf16[128,20,128]{0,2,1:T(8,128)(2,1)}), bf16[128,20,128]{0,2,1:T(8,128)(2,1)S(1)}, u32[]{:S(2)}, u32[]{:S(2)}) async-start(bf16[128,20,128]{0,2,1:T(8,128)(2,1)} %bitcast.73), calls=%async_computation | async-start | bytes 1310720 | tf_op jit(solution)/shard_map/all_to_all | solution.py:63
  30.3 13.7 %all-to-all-start.1 = ((bf16[128,20,128]{0,2,1:T(8,128)(2,1)}), bf16[128,20,128]{0,2,1:T(8,128)(2,1)S(1)}, u32[]{:S(2)}, u32[]{:S(2)}) async-start(bf16[128,20,128]{0,2,1:T(8,128)(2,1)} %bitcast.74), calls=%async_computation.1 | async-start | bytes 1310720 | tf_op jit(solution)/shard_map/all_to_all | solution.py:77
  56.6 13.7 %all-to-all-start.5 = ((bf16[128,20,128]{0,2,1:T(8,128)(2,1)}), bf16[128,20,128]{0,2,1:T(8,128)(2,1)S(1)}, u32[]{:S(2)}, u32[]{:S(2)}) async-start(bf16[128,20,128]{0,2,1:T(8,128)(2,1)} %bitcast.72), calls=%async_computation.5 | async-start | bytes 1310720 | tf_op jit(solution)/shard_map/all_to_all | solution.py:70
  70.2 14.5 %all-to-all-start.6 = ((bf16[128,20,128]{0,2,1:T(8,128)(2,1)}), bf16[128,20,128]{0,2,1:T(8,128)(2,1)S(1)}, u32[]{:S(2)}, u32[]{:S(2)}) async-start(bf16[128,20,128]{0,2,1:T(8,128)(2,1)} %bitcast.71), calls=%async_computation.6 | async-start | bytes 1310720 | tf_op jit(solution)/shard_map/all_to_all | solution.py:84
  84.8 4.9 slice-start
  85.9 4.0 slice-start.1
  85.9 4.1 copy-start.2
  85.9 4.3 copy-start.4
  85.9 8.2 slice-start.2
  90.2 3.9 copy-start.3
  90.2 3.9 slice-start.3
  96.8 17.9 %all-to-all-start.7 = ((bf16[512,5,128]{2,1,0:T(8,128)(2,1)}), bf16[512,5,128]{2,1,0:T(8,128)(2,1)S(1)}, u32[]{:S(2)}, u32[]{:S(2)}) async-start(bf16[512,5,128]{2,1,0:T(8,128)(2,1)} %copy.85), calls=%async_computation.7 | async-start | bytes 2097152 | tf_op jit(solution)/shard_map/all_to_all | solution.py:106
  103.9 14.4 %copy-start.5 = (bf16[640,80]{0,1:T(8,128)(2,1)S(1)}, bf16[640,80]{0,1:T(8,128)(2,1)}, u32[]{:S(2)}) copy-start(bf16[640,80]{0,1:T(8,128)(2,1)} %param.17) | copy-start | bytes 307204
  114.7 21.0 %all-to-all-start.3 = ((bf16[512,5,128]{2,1,0:T(8,128)(2,1)}), bf16[512,5,128]{2,1,0:T(8,128)(2,1)S(1)}, u32[]{:S(2)}, u32[]{:S(2)}) async-start(bf16[512,5,128]{2,1,0:T(8,128)(2,1)} %copy.71), calls=%async_computation.3 | async-start | bytes 2097152 | tf_op jit(solution)/shard_map/all_to_all | solution.py:105
  144.5 684.2 %all-to-all-start.8 = ((bf16[64,2560,80]{1,2,0:T(8,128)(2,1)}), bf16[64,2560,80]{1,2,0:T(8,128)(2,1)}, u32[]{:S(2)}, u32[]{:S(2)}) async-start(bf16[64,2560,80]{1,2,0:T(8,128)(2,1)} %stack.2), calls=%async_computation.8 | async-start | bytes 52428800 | tf_op jit(solution)/shard_map/all_to_all | solution.py:115
